TPU v7x, 32 devices: a whole 2x2x4 slice. The times are simulated.
32 devices in a mesh: groups: 2 (over y), seq: 4 (over z), inner: 2 (over x), batch: 2 (over core).
Axes of the slice: x: 2, y: 2, z: 4, core: 2. Of those that a mesh axis runs over, the one named last changes fastest.
Arguments:
- queries: bfloat16 [4, 2048, 256], P(('groups', 'batch'), ('seq', 'inner')), parts along dimension 0, may hold values from -6 to 6
- keys: bfloat16 [4, 2048, 256], P(('groups', 'batch'), ('seq', 'inner')), parts along dimension 0, may hold values from -6 to 6
- values: bfloat16 [4, 2048, 256], P(('groups', 'batch'), ('seq', 'inner')), parts along dimension 0, may hold values from -6 to 6
- rates: float32 [4, 2048], P(('groups', 'batch'), ('seq', 'inner')), parts along dimension 0, may hold values from 0.05 to 1
- video_start: int32 [4], P(('groups', 'batch')), parts along dimension 0, may hold values from 0 to 511
- span_len: int32 [4, 4], P(('groups', 'batch'), 'seq'), parts along dimension 0, may hold values from 256 to 512, as said below
- init_weights: float32 [3, 256, 256], replicated, may hold values from -0.375 to 0.375
Outputs:
- outputs: bfloat16 [4, 2048, 256], P(('groups', 'batch'), ('seq', 'inner')), parts along dimension 0
- final_weights: float32 [4, 3, 256, 256], P(('groups', 'batch'), None, 'seq'), parts along dimension 0
There are 2 independent parts, one for each index of `groups`. A program takes and returns all parts, laid end to end along the dimension named above; an argument that names none is the same for every part. Nothing has to cross between parts.
Inputs may be any that keep to these rules, and one draw needn't show every extreme that they name: Every video has at least one span with span_len equal to 512.
All inputs are finite; a program needn't handle non-finite values.
Results may differ from a plain program's by a relative error of at most 0.015.
Values may be sent and summed in bfloat16 or wider, within the bound.
A program may use at most 64 MiB of HBM per device.

v0:
```python
import jax
import jax.numpy as jnp
from jax import lax
from jax.sharding import PartitionSpec as P

NS_STEPS = 5
step_size = 0.1
norm_eps = 1e-07
column_eps = 1e-06


def shifted(value, axis, steps):
    count = lax.axis_size(axis)
    initial, last = (max(0, -steps), min(count, count - steps))
    return lax.ppermute(value, axis, [(source, source + steps) for source in range(initial, last)])


def broadcast(value, axis, root):
    mine = lax.axis_index(axis) == root
    return lax.psum(jnp.where(mine, value, jnp.zeros_like(value)), axis)


def swish_parts(pre_act):
    sigma = jax.nn.sigmoid(pre_act)
    return (pre_act * sigma, sigma * (1.0 + pre_act * (1.0 - sigma)))


def apply_net(rows, half_weights):
    gate_pre = jnp.dot(rows, half_weights[0], preferred_element_type=jnp.float32)
    up_pre = jnp.dot(rows, half_weights[1], preferred_element_type=jnp.float32)
    active_part, unused_slope = swish_parts(gate_pre)
    hidden = (active_part * up_pre).astype(jnp.bfloat16)
    contract = (((1,), (1,)), ((), ()))
    return lax.dot_general(
        hidden, half_weights[2], contract, preferred_element_type=jnp.float32
    ).astype(jnp.bfloat16)


def key_grads(key_rows, value_rows, weight, half_weights):
    gate_pre = jnp.dot(key_rows, half_weights[0], preferred_element_type=jnp.float32)
    up_pre = jnp.dot(key_rows, half_weights[1], preferred_element_type=jnp.float32)
    active_part, slope_term = swish_parts(gate_pre)
    hidden = (active_part * up_pre).astype(jnp.bfloat16)
    neg_values = (-(weight[:, None] * value_rows.astype(jnp.float32))).astype(jnp.bfloat16)
    back_grad = jnp.dot(neg_values, half_weights[2], preferred_element_type=jnp.float32)
    d_upper = (back_grad * active_part).astype(jnp.bfloat16)
    d_gate = (back_grad * up_pre * slope_term).astype(jnp.bfloat16)
    contract = (((0,), (0,)), ((), ()))
    grad_one = lax.dot_general(key_rows, d_gate, contract, preferred_element_type=jnp.float32)
    grad_three = lax.dot_general(key_rows, d_upper, contract, preferred_element_type=jnp.float32)
    grad_two = lax.dot_general(neg_values, hidden, contract, preferred_element_type=jnp.float32)
    return jnp.stack([grad_one, grad_three, grad_two])


def newton(grad):
    scale = jnp.sqrt(jnp.sum(grad * grad))
    iterate = grad / (scale + norm_eps)
    for unused in range(NS_STEPS):
        gram = jnp.dot(
            iterate, iterate.T, precision=lax.Precision.HIGHEST, preferred_element_type=jnp.float32
        )
        iterate = 1.5 * iterate - 0.5 * jnp.dot(
            gram, iterate, precision=lax.Precision.HIGHEST, preferred_element_type=jnp.float32
        )
    return iterate.astype(jnp.bfloat16)


def renorm(before, moved):
    old_norm = jnp.sqrt(jnp.sum(before * before, axis=1, keepdims=True) + column_eps)
    new_norm = jnp.sqrt(jnp.sum(moved * moved, axis=1, keepdims=True) + column_eps)
    return moved * (old_norm / new_norm)


def ortho_all(total):
    return jax.vmap(newton)(total)


def ortho_none(total):
    return jnp.zeros(total.shape, jnp.bfloat16)


def pad_slots(array, slot_total):
    filler = jnp.zeros((slot_total - array.shape[0],) + tuple(array.shape[1:]), array.dtype)
    return jnp.concatenate([array, filler], axis=0)


def per_device(queries, keys, values, rates, video_start, span_len, init_weights):
    video_count, tok_rows, head_width = queries.shape
    seq_count = lax.axis_size("seq")
    inner_count = lax.axis_size("inner")
    seq_place = lax.axis_index("seq")
    inner_place = lax.axis_index("inner")
    span_rows = tok_rows * inner_count
    within = jnp.arange(tok_rows, dtype=jnp.int32) + inner_place * tok_rows
    state_shape = init_weights.shape
    per_owner = (state_shape[0] + inner_count - 1) // inner_count
    slot_total = per_owner * inner_count

    def local_terms(video_slot, state):
        half_weights = state.astype(jnp.bfloat16)
        query_rows = lax.dynamic_index_in_dim(queries, video_slot, 0, keepdims=False)
        key_rows = lax.dynamic_index_in_dim(keys, video_slot, 0, keepdims=False)
        value_rows = lax.dynamic_index_in_dim(values, video_slot, 0, keepdims=False)
        rate_rows = lax.dynamic_index_in_dim(rates, video_slot, 0, keepdims=False)
        length = lax.dynamic_index_in_dim(span_len, video_slot, 0, keepdims=False)[0]
        begin = lax.dynamic_index_in_dim(video_start, video_slot, 0, keepdims=False)
        position = seq_place * span_rows + within
        valid = ((position >= begin) & (within < length)).astype(jnp.float32)
        weight = rate_rows * valid
        partial_value = (
            key_grads(key_rows, value_rows, weight, half_weights)
            .astype(jnp.bfloat16)
            .astype(jnp.float32)
        )
        return (apply_net(query_rows, half_weights), partial_value)

    def skip_terms(video_slot, state):
        return (
            jnp.zeros((tok_rows, head_width), jnp.bfloat16),
            jnp.zeros(state_shape, jnp.float32),
        )

    final_shape = (video_count,) + tuple(state_shape)

    def step(turn_index, carry):
        incoming, outputs, finals = carry
        video_index = turn_index - seq_place
        active = (video_index >= 0) & (video_index < video_count)
        video_slot = jnp.clip(video_index, 0, video_count - 1)
        state = jnp.where(seq_place == 0, init_weights, incoming)
        out_rows, partial_value = lax.cond(active, local_terms, skip_terms, video_slot, state)
        padded = pad_slots(partial_value, slot_total)
        owned = lax.psum_scatter(
            padded.astype(jnp.bfloat16), "inner", scatter_dimension=0, tiled=True
        ).astype(jnp.float32)
        mine = lax.cond(active, ortho_all, ortho_none, owned)
        ortho = lax.all_gather(mine, "inner", axis=0, tiled=True)[: state_shape[0]]
        old_out = lax.dynamic_index_in_dim(outputs, video_slot, 0, keepdims=False)
        outputs = lax.dynamic_update_index_in_dim(
            outputs, jnp.where(active, out_rows, old_out), video_slot, 0
        )
        store = active & (seq_place == seq_count - 1)
        old_final = lax.dynamic_index_in_dim(finals, video_slot, 0, keepdims=False)
        new_state = renorm(state, state - step_size * ortho.astype(jnp.float32))
        finals = lax.dynamic_update_index_in_dim(
            finals, jnp.where(store, new_state, old_final), video_slot, 0
        )
        incoming = shifted(new_state, "seq", 1)
        return (incoming, outputs, finals)

    start_carry = (
        jnp.zeros(state_shape, jnp.float32),
        jnp.zeros(queries.shape, jnp.bfloat16),
        jnp.zeros(final_shape, jnp.float32),
    )
    last_in, outputs, finals = lax.fori_loop(0, video_count + seq_count - 1, step, start_carry)
    everything = broadcast(finals, "seq", seq_count - 1)
    row_count = head_width // seq_count
    return (outputs, lax.dynamic_slice_in_dim(everything, seq_place * row_count, row_count, 2))


def solution(mesh):
    in_specs = (
        P(("groups", "batch"), ("seq", "inner"), None),
        P(("groups", "batch"), ("seq", "inner"), None),
        P(("groups", "batch"), ("seq", "inner"), None),
        P(("groups", "batch"), ("seq", "inner")),
        P(("groups", "batch")),
        P(("groups", "batch"), "seq"),
        P(),
    )
    out_specs = (
        P(("groups", "batch"), ("seq", "inner"), None),
        P(("groups", "batch"), None, "seq", None),
    )
    return jax.shard_map(
        per_device, mesh=mesh, in_specs=in_specs, out_specs=out_specs, check_vma=False
    )
```

profile of v0, /device:TPU:0, one launch (start us, length us, event | category | flops | bytes accessed | tf_op | source)
XLA Modules:
  0.0 295.1 jit_solution(18334689422847363460)
XLA Ops:
  8.2 1.0 copy-done
  9.2 222.7 %while.19 = (s32[]{:T(128)}, f32[3,256,256]{2,1,0:T(8,128)S(1)}, bf16[1,256,256]{2,1,0:T(8,128)(2,1)S(1)}, f32[1,3,256,256]{3,2,1,0:T(8,128)S(1)}, pred[]{:T(512...) while((s32[]{:T(128)}, f32[3,256,256]{2,1,0:T(8,128)S(1)}, ...), condition=%wide.region_9.10_spmd.clone, body=%wide.region_0.9_spmd.clone.sunk | while | flops 4337240064 | bytes 41312808 | solution.py:156
  9.3 5.0 %conditional.6 = (bf16[256,256]{1,0:T(8,128)(2,1)S(1)}, bf16[3,256,256]{1,2,0:T(8,128)(2,1)S(1)}) conditional(s32[]{:T(128)} %convert_element_type.135, () %tuple.73, (bf16[1,256,256]{2,1,0:T(8,128)(2,1)}, f32[3,256,256]{2,1,0:T(8,128)S(1)}, s32[]{:T(128)}, s32[256]{0:T(256)S(1)}, s32[1]{0:T(128)}, /*index=5*/s32[1,1]{1,0:T(1,128)}, ...), branch_computations={%region_1.1_spmd, %region_2.2_spmd} | conditional | flops 305202688 | bytes 8524900 | solution.py:131
  9.4 1.3 and_select_fusion
  10.9 0.7 copy-done.5
  13.0 0.8 copy-done.4
  14.5 0.8 concatenate.7
  15.4 14.5 %reduce-scatter.2.cloned.1.call-done = bf16[2,256,256]{2,1,0:T(8,128)(2,1)} async-done(((bf16[4,256,256]{2,1,0:T(8,128)(2,1)}), bf16[2,256,256]{2,1,0:T(8,128)(2,1)}) %reduce-scatter.2.cloned.1.call-update) | async-done | bytes 262160 | tf_op jit(solution)/shard_map/while/body/eval_jaxpr/reduce_scatter | solution.py:133
  29.8 1.0 convert_element_type.136
  30.8 7.2 %conditional.7 = (bf16[2,256,256]{2,1,0:T(8,128)(2,1)S(1)}) conditional(s32[]{:T(128)} %convert_element_type.135, () %tuple.72, f32[2,256,256]{2,1,0:T(8,128)S(1)} %convert_element_type.136), branch_computations={%region_4.4_spmd, %region_5.6_spmd} | conditional | flops 4029284352 | bytes 13369392 | solution.py:136
  31.0 0.8 fusion.46
  31.8 0.8 fusion.44
  32.6 0.7 fusion.51
  33.2 0.7 fusion.43
  33.9 0.7 fusion.52
  34.6 0.7 fusion.42
  35.3 0.7 fusion.53
  35.9 0.7 fusion.41
  36.6 0.7 fusion.54
  37.3 0.7 fusion.45
  38.0 8.6 %all_gather.10 = bf16[4,256,256]{2,1,0:T(8,128)(2,1)S(1)} all-gather(bf16[2,256,256]{2,1,0:T(8,128)(2,1)S(1)} %get-tuple-element.569), channel_id=1, replica_groups=mesh['groups'=2,'seq'=4,'inner'=2,'batch'=2] {'inner'}, dimensions={0}, use_global_device_ids=true | all-gather | bytes 786432 | tf_op jit(solution)/shard_map/while/body/eval_jaxpr/all_gather | solution.py:137
  46.8 1.3 fusion.74
  48.0 1.3 collective-permute-start
  49.4 16.3 %collective-permute-done = f32[3,256,256]{2,1,0:T(8,128)S(1)} collective-permute-done((f32[3,256,256]{2,1,0:T(8,128)}, f32[3,256,256]{2,1,0:T(8,128)S(1)}, u32[]{:S(2)}, u32[]{:S(2)}) %collective-permute-start) | collective-permute-done | bytes 786464 | tf_op jit(solution)/shard_map/while/body/eval_jaxpr/ppermute | solution.py:15
  66.0 0.8 concatenate.7
  66.9 18.8 %reduce-scatter.2.cloned.1.call-done = bf16[2,256,256]{2,1,0:T(8,128)(2,1)} async-done(((bf16[4,256,256]{2,1,0:T(8,128)(2,1)}), bf16[2,256,256]{2,1,0:T(8,128)(2,1)}) %reduce-scatter.2.cloned.1.call-update) | async-done | bytes 262160 | tf_op jit(solution)/shard_map/while/body/eval_jaxpr/reduce_scatter | solution.py:133
  85.7 1.0 convert_element_type.136
  86.7 8.6 %all_gather.10 = bf16[4,256,256]{2,1,0:T(8,128)(2,1)S(1)} all-gather(bf16[2,256,256]{2,1,0:T(8,128)(2,1)S(1)} %get-tuple-element.569), channel_id=1, replica_groups=mesh['groups'=2,'seq'=4,'inner'=2,'batch'=2] {'inner'}, dimensions={0}, use_global_device_ids=true | all-gather | bytes 786432 | tf_op jit(solution)/shard_map/while/body/eval_jaxpr/all_gather | solution.py:137
  95.5 1.3 fusion.74
  96.8 10.5 %collective-permute-start = (f32[3,256,256]{2,1,0:T(8,128)}, f32[3,256,256]{2,1,0:T(8,128)S(1)}, u32[]{:S(2)}, u32[]{:S(2)}) collective-permute-start(f32[3,256,256]{2,1,0:T(8,128)} %get-tuple-element.508), channel_id=1, source_target_pairs={{0,4},{4,8},{8,12},{1,5},{5,9},{9,13},{2,6},{6,10},{10,14},{3,7},{... | collective-permute-start | bytes 2359304 | tf_op jit(solution)/shard_map/while/body/eval_jaxpr/ppermute | solution.py:15
  107.3 16.0 %collective-permute-done = f32[3,256,256]{2,1,0:T(8,128)S(1)} collective-permute-done((f32[3,256,256]{2,1,0:T(8,128)}, f32[3,256,256]{2,1,0:T(8,128)S(1)}, u32[]{:S(2)}, u32[]{:S(2)}) %collective-permute-start) | collective-permute-done | bytes 786464 | tf_op jit(solution)/shard_map/while/body/eval_jaxpr/ppermute | solution.py:15
  123.7 0.8 concatenate.7
  124.5 18.5 %reduce-scatter.2.cloned.1.call-done = bf16[2,256,256]{2,1,0:T(8,128)(2,1)} async-done(((bf16[4,256,256]{2,1,0:T(8,128)(2,1)}), bf16[2,256,256]{2,1,0:T(8,128)(2,1)}) %reduce-scatter.2.cloned.1.call-update) | async-done | bytes 262160 | tf_op jit(solution)/shard_map/while/body/eval_jaxpr/reduce_scatter | solution.py:133
  143.1 1.0 convert_element_type.136
  144.1 8.6 %all_gather.10 = bf16[4,256,256]{2,1,0:T(8,128)(2,1)S(1)} all-gather(bf16[2,256,256]{2,1,0:T(8,128)(2,1)S(1)} %get-tuple-element.569), channel_id=1, replica_groups=mesh['groups'=2,'seq'=4,'inner'=2,'batch'=2] {'inner'}, dimensions={0}, use_global_device_ids=true | all-gather | bytes 786432 | tf_op jit(solution)/shard_map/while/body/eval_jaxpr/all_gather | solution.py:137
  152.9 1.3 fusion.74
  154.1 3.4 %collective-permute-start = (f32[3,256,256]{2,1,0:T(8,128)}, f32[3,256,256]{2,1,0:T(8,128)S(1)}, u32[]{:S(2)}, u32[]{:S(2)}) collective-permute-start(f32[3,256,256]{2,1,0:T(8,128)} %get-tuple-element.508), channel_id=1, source_target_pairs={{0,4},{4,8},{8,12},{1,5},{5,9},{9,13},{2,6},{6,10},{10,14},{3,7},{... | collective-permute-start | bytes 2359304 | tf_op jit(solution)/shard_map/while/body/eval_jaxpr/ppermute | solution.py:15
  157.6 16.0 %collective-permute-done = f32[3,256,256]{2,1,0:T(8,128)S(1)} collective-permute-done((f32[3,256,256]{2,1,0:T(8,128)}, f32[3,256,256]{2,1,0:T(8,128)S(1)}, u32[]{:S(2)}, u32[]{:S(2)}) %collective-permute-start) | collective-permute-done | bytes 786464 | tf_op jit(solution)/shard_map/while/body/eval_jaxpr/ppermute | solution.py:15
  174.0 0.8 concatenate.7
  174.8 26.5 %reduce-scatter.2.cloned.1.call-done = bf16[2,256,256]{2,1,0:T(8,128)(2,1)} async-done(((bf16[4,256,256]{2,1,0:T(8,128)(2,1)}), bf16[2,256,256]{2,1,0:T(8,128)(2,1)}) %reduce-scatter.2.cloned.1.call-update) | async-done | bytes 262160 | tf_op jit(solution)/shard_map/while/body/eval_jaxpr/reduce_scatter | solution.py:133
  201.4 1.0 convert_element_type.136
  202.4 8.5 %all_gather.10 = bf16[4,256,256]{2,1,0:T(8,128)(2,1)S(1)} all-gather(bf16[2,256,256]{2,1,0:T(8,128)(2,1)S(1)} %get-tuple-element.569), channel_id=1, replica_groups=mesh['groups'=2,'seq'=4,'inner'=2,'batch'=2] {'inner'}, dimensions={0}, use_global_device_ids=true | all-gather | bytes 786432 | tf_op jit(solution)/shard_map/while/body/eval_jaxpr/all_gather | solution.py:137
  211.2 1.3 fusion.74
  212.4 3.4 %collective-permute-start = (f32[3,256,256]{2,1,0:T(8,128)}, f32[3,256,256]{2,1,0:T(8,128)S(1)}, u32[]{:S(2)}, u32[]{:S(2)}) collective-permute-start(f32[3,256,256]{2,1,0:T(8,128)} %get-tuple-element.508), channel_id=1, source_target_pairs={{0,4},{4,8},{8,12},{1,5},{5,9},{9,13},{2,6},{6,10},{10,14},{3,7},{... | collective-permute-start | bytes 2359304 | tf_op jit(solution)/shard_map/while/body/eval_jaxpr/ppermute | solution.py:15
  215.9 16.0 %collective-permute-done = f32[3,256,256]{2,1,0:T(8,128)S(1)} collective-permute-done((f32[3,256,256]{2,1,0:T(8,128)}, f32[3,256,256]{2,1,0:T(8,128)S(1)}, u32[]{:S(2)}, u32[]{:S(2)}) %collective-permute-start) | collective-permute-done | bytes 786464 | tf_op jit(solution)/shard_map/while/body/eval_jaxpr/ppermute | solution.py:15
  231.9 1.0 broadcast_select_fusion.1
  232.9 53.5 %all-reduce.3.cloned.1.call-done = f32[1,3,256,256]{3,2,1,0:T(8,128)} async-done(((f32[1,3,256,256]{3,2,1,0:T(8,128)}), f32[1,3,256,256]{3,2,1,0:T(8,128)}) %all-reduce.3.cloned.1.call-update) | async-done | bytes 786448 | tf_op jit(solution)/shard_map/psum | solution.py:20
  286.4 1.6 constant_dynamic-slice_fusion
  (81 shorter events, 5.2 us)
Async XLA Ops:
  8.0 1.1 copy-start
  8.1 1.1 copy-start.2
  8.1 1.1 copy-start.6
  9.2 20.6 %reduce-scatter.2.cloned.1.call-start = ((), (), s32[]{:S(2)}) async-start(), calls=%async_computation.2 | async-start | bytes 786432 | tf_op jit(solution)/shard_map/while/body/eval_jaxpr/reduce_scatter | solution.py:133
  10.7 0.9 copy-start.5
  12.9 0.9 copy-start.4
  46.8 18.9 %copy-start.1 = (f32[3,256,256]{2,1,0:T(8,128)S(1)}, f32[3,256,256]{2,1,0:T(8,128)}, u32[]{:S(2)}) copy-start(f32[3,256,256]{2,1,0:T(8,128)} %get-tuple-element.593) | copy-start | bytes 2359300 | tf_op jit(solution)/shard_map/while
  48.0 17.6 %collective-permute-start = (f32[3,256,256]{2,1,0:T(8,128)}, f32[3,256,256]{2,1,0:T(8,128)S(1)}, u32[]{:S(2)}, u32[]{:S(2)}) collective-permute-start(f32[3,256,256]{2,1,0:T(8,128)} %get-tuple-element.508), channel_id=1, source_target_pairs={{0,4},{4,8},{8,12},{1,5},{5,9},{9,13},{2,6},{6,10},{10,14},{3,7},{... | collective-permute-start | bytes 2359304 | tf_op jit(solution)/shard_map/while/body/eval_jaxpr/ppermute | solution.py:15
  65.7 20.0 %reduce-scatter.2.cloned.1.call-start = ((), (), s32[]{:S(2)}) async-start(), calls=%async_computation.2 | async-start | bytes 786432 | tf_op jit(solution)/shard_map/while/body/eval_jaxpr/reduce_scatter | solution.py:133
  95.5 27.8 %copy-start.1 = (f32[3,256,256]{2,1,0:T(8,128)S(1)}, f32[3,256,256]{2,1,0:T(8,128)}, u32[]{:S(2)}) copy-start(f32[3,256,256]{2,1,0:T(8,128)} %get-tuple-element.593) | copy-start | bytes 2359300 | tf_op jit(solution)/shard_map/while
  96.8 26.5 %collective-permute-start = (f32[3,256,256]{2,1,0:T(8,128)}, f32[3,256,256]{2,1,0:T(8,128)S(1)}, u32[]{:S(2)}, u32[]{:S(2)}) collective-permute-start(f32[3,256,256]{2,1,0:T(8,128)} %get-tuple-element.508), channel_id=1, source_target_pairs={{0,4},{4,8},{8,12},{1,5},{5,9},{9,13},{2,6},{6,10},{10,14},{3,7},{... | collective-permute-start | bytes 2359304 | tf_op jit(solution)/shard_map/while/body/eval_jaxpr/ppermute | solution.py:15
  123.3 19.8 %reduce-scatter.2.cloned.1.call-start = ((), (), s32[]{:S(2)}) async-start(), calls=%async_computation.2 | async-start | bytes 786432 | tf_op jit(solution)/shard_map/while/body/eval_jaxpr/reduce_scatter | solution.py:133
  152.9 20.7 %copy-start.1 = (f32[3,256,256]{2,1,0:T(8,128)S(1)}, f32[3,256,256]{2,1,0:T(8,128)}, u32[]{:S(2)}) copy-start(f32[3,256,256]{2,1,0:T(8,128)} %get-tuple-element.593) | copy-start | bytes 2359300 | tf_op jit(solution)/shard_map/while
  154.1 19.5 %collective-permute-start = (f32[3,256,256]{2,1,0:T(8,128)}, f32[3,256,256]{2,1,0:T(8,128)S(1)}, u32[]{:S(2)}, u32[]{:S(2)}) collective-permute-start(f32[3,256,256]{2,1,0:T(8,128)} %get-tuple-element.508), channel_id=1, source_target_pairs={{0,4},{4,8},{8,12},{1,5},{5,9},{9,13},{2,6},{6,10},{10,14},{3,7},{... | collective-permute-start | bytes 2359304 | tf_op jit(solution)/shard_map/while/body/eval_jaxpr/ppermute | solution.py:15
  173.6 27.8 %reduce-scatter.2.cloned.1.call-start = ((), (), s32[]{:S(2)}) async-start(), calls=%async_computation.2 | async-start | bytes 786432 | tf_op jit(solution)/shard_map/while/body/eval_jaxpr/reduce_scatter | solution.py:133
  211.1 20.8 %copy-start.1 = (f32[3,256,256]{2,1,0:T(8,128)S(1)}, f32[3,256,256]{2,1,0:T(8,128)}, u32[]{:S(2)}) copy-start(f32[3,256,256]{2,1,0:T(8,128)} %get-tuple-element.593) | copy-start | bytes 2359300 | tf_op jit(solution)/shard_map/while
  212.4 19.5 %collective-permute-start = (f32[3,256,256]{2,1,0:T(8,128)}, f32[3,256,256]{2,1,0:T(8,128)S(1)}, u32[]{:S(2)}, u32[]{:S(2)}) collective-permute-start(f32[3,256,256]{2,1,0:T(8,128)} %get-tuple-element.508), channel_id=1, source_target_pairs={{0,4},{4,8},{8,12},{1,5},{5,9},{9,13},{2,6},{6,10},{10,14},{3,7},{... | collective-permute-start | bytes 2359304 | tf_op jit(solution)/shard_map/while/body/eval_jaxpr/ppermute | solution.py:15
  231.9 1.0 copy-start.3
  231.9 54.5 %all-reduce.3.cloned.1.call-start = ((), (), s32[]{:S(2)}) async-start(), calls=%async_computation.1 | async-start | bytes 1572864 | tf_op jit(solution)/shard_map/psum | solution.py:20
Sparse Core Ops, SparseCore 0:
  15.5 14.2 reduce-scatter.1
  68.7 16.9 reduce-scatter.1
  126.3 16.6 reduce-scatter.1
  176.3 24.9 reduce-scatter.1
Sparse Core Ops, SparseCore 1:
  234.7 51.6 all-reduce.2
where the time goes:
time: 296 us; the launch traced here: 295 us
  waiting for transfers between devices  196 us (66%)
  blocking collectives  34.2 us (12%)
  starting transfers between devices  18.7 us (6%)
  between operations  15.2 us (5%)
  other arithmetic  12.9 us (4%)
  matrix products  8.87 us (3%)
  local copies, waits for them, and re-layouts  8.5 us (3%)
    reduce_scatter x4, waiting for transfers between devices, step(): lax.psum_scatter(padded.astype(jnp.bfloat16), 'inner', scatter_dimension=...  78.3 us
    ppermute x4, waiting for transfers between devices, shifted(): lax.ppermute(value, axis, [(source, source + steps) for source in range(i...  64.2 us
    psum x1, waiting for transfers between devices, broadcast(): return lax.psum(jnp.where(mine, value, jnp.zeros_like(value)), axis)  53.5 us
    all_gather x4, blocking collectives, step(): ortho = lax.all_gather(mine, 'inner', axis=0, tiled=True)[:state_shape[0]]  34.2 us
    ppermute x4, starting transfers between devices, shifted(): lax.ppermute(value, axis, [(source, source + steps) for source in range(i...  18.7 us
  transfers between devices with their start and end apart: 9, of which 9 were waited for; matrix products, arithmetic and copies ran while one was open for 0% of the time, Pallas kernels for 0%

commit v1 on v0

--- a/solution.py
+++ b/solution.py
@@ -7,6 +7,18 @@
 step_size = 0.1
 norm_eps = 1e-07
 column_eps = 1e-06
+
+
+def doubled_up(shard, axis, dim):
+    ways, here = (lax.axis_size(axis), lax.axis_index(axis))
+    grown, reach = (shard, 1)
+    while reach < ways:
+        theirs = lax.ppermute(grown, axis, [(d, d ^ reach) for d in range(ways)])
+        mine_first = jnp.concatenate([grown, theirs], axis=dim)
+        theirs_first = jnp.concatenate([theirs, grown], axis=dim)
+        grown = jnp.where(here & reach == 0, mine_first, theirs_first)
+        reach = 2 * reach
+    return grown
 
 
 def shifted(value, axis, steps):
@@ -134,7 +146,7 @@
             padded.astype(jnp.bfloat16), "inner", scatter_dimension=0, tiled=True
         ).astype(jnp.float32)
         mine = lax.cond(active, ortho_all, ortho_none, owned)
-        ortho = lax.all_gather(mine, "inner", axis=0, tiled=True)[: state_shape[0]]
+        ortho = doubled_up(mine, "inner", 0)[: state_shape[0]]
         old_out = lax.dynamic_index_in_dim(outputs, video_slot, 0, keepdims=False)
         outputs = lax.dynamic_update_index_in_dim(
             outputs, jnp.where(active, out_rows, old_out), video_slot, 0

time: 296 us -> 289 us (0.976)
  blocking collectives: 34.2 us -> 0 us
  waiting for transfers between devices: 196 us -> 218 us
  other arithmetic: 12.9 us -> 17.7 us
    all_gather x4 -> x0, blocking collectives: 34.2 us -> none  [step(): ortho = lax.all_gather(mine, 'inner', axis=0, tiled=True)[:state_shape[0]]]
    ppermute x0 -> x4, waiting for transfers between devices: none -> 30.1 us  [doubled_up(): theirs = lax.ppermute(grown, axis, [(d, d ^ reach) for d in range(ways)])]
    reduce_scatter x4, waiting for transfers between devices: 78.3 us -> 70.4 us  [step(): lax.psum_scatter(padded.astype(jnp.bfloat16), 'inner', scatter_dimension=...]
    select_n x4, other arithmetic: 0.4 us -> 4.94 us  [step(): state = jnp.where(seq_place == 0, init_weights, incoming)]
  transfers between devices with their start and end apart: 9 -> 13, of which waited for: 9 -> 13; matrix products, arithmetic and copies ran while one was open for 0% -> 0% of each run, Pallas kernels for 0% -> 0%
where the time goes in v1:
time: 289 us; the launch traced here: 288 us
  waiting for transfers between devices  218 us (75%)
  starting transfers between devices  20.4 us (7%)
  other arithmetic  17.7 us (6%)
  between operations  15.2 us (5%)
  matrix products  8.87 us (3%)
  local copies, waits for them, and re-layouts  6.91 us (2%)
    reduce_scatter x4, waiting for transfers between devices, step(): lax.psum_scatter(padded.astype(jnp.bfloat16), 'inner', scatter_dimension=...  70.4 us
    ppermute x4, waiting for transfers between devices, shifted(): lax.ppermute(value, axis, [(source, source + steps) for source in range(i...  64.2 us
    psum x1, waiting for transfers between devices, broadcast(): return lax.psum(jnp.where(mine, value, jnp.zeros_like(value)), axis)  53.5 us
    ppermute x4, waiting for transfers between devices, doubled_up(): theirs = lax.ppermute(grown, axis, [(d, d ^ reach) for d in range(ways)])  30.1 us
    ppermute x4, starting transfers between devices, shifted(): lax.ppermute(value, axis, [(source, source + steps) for source in range(i...  18.8 us
  transfers between devices with their start and end apart: 13, of which 13 were waited for; matrix products, arithmetic and copies ran while one was open for 0% of the time, Pallas kernels for 0%

profile of v1, /device:TPU:0, one launch (start us, length us, event | category | flops | bytes accessed | tf_op | source)
XLA Modules:
  0.0 288.0 jit_solution(16502594014466152601)
XLA Ops:
  8.2 0.8 copy-done
  9.1 215.7 %while.19 = (s32[]{:T(128)}, f32[3,256,256]{2,1,0:T(8,128)S(1)}, bf16[1,256,256]{2,1,0:T(8,128)(2,1)S(1)}, f32[1,3,256,256]{3,2,1,0:T(8,128)S(1)}, pred[]{:T(512...) while((s32[]{:T(128)}, f32[3,256,256]{2,1,0:T(8,128)S(1)}, ...), condition=%wide.region_9.10_spmd.clone, body=%wide.region_0.9_spmd.clone.sunk | while | flops 4338419712 | bytes 37642800 | solution.py:168
  9.1 1.2 broadcast_select_fusion.3
  10.4 3.5 %conditional.6 = (bf16[256,256]{1,0:T(8,128)(2,1)S(1)}, bf16[3,256,256]{1,2,0:T(8,128)(2,1)S(1)}) conditional(s32[]{:T(128)} %convert_element_type.135, () %tuple.73, (bf16[1,256,256]{2,1,0:T(8,128)(2,1)S(1)}, f32[3,256,256]{2,1,0:T(8,128)S(1)}, s32[]{:T(128)}, s32[256]{0:T(256)S(1)}, s32[1]{0:T(128)}, /*index=5*/s32[1,1]{1,0:T(1,128)}, ...), branch_computations={%region_1.1_spmd, %region_2.2_spmd} | conditional | flops 305202688 | bytes 7476268 | solution.py:143
  10.5 1.3 and_select_fusion
  14.0 0.8 concatenate.25
  14.9 14.7 %reduce-scatter.2.cloned.1.call-done = bf16[2,256,256]{2,1,0:T(8,128)(2,1)} async-done(((bf16[4,256,256]{2,1,0:T(8,128)(2,1)}), bf16[2,256,256]{2,1,0:T(8,128)(2,1)}) %reduce-scatter.2.cloned.1.call-update) | async-done | bytes 262160 | tf_op jit(solution)/shard_map/while/body/eval_jaxpr/reduce_scatter | solution.py:145
  29.5 1.0 convert_element_type.136
  30.5 7.2 %conditional.7 = (bf16[2,256,256]{2,1,0:T(8,128)(2,1)S(1)}) conditional(s32[]{:T(128)} %convert_element_type.135, () %tuple.72, f32[2,256,256]{2,1,0:T(8,128)S(1)} %convert_element_type.136), branch_computations={%region_4.4_spmd, %region_5.6_spmd} | conditional | flops 4029284352 | bytes 13369392 | solution.py:148
  30.7 0.8 fusion.46
  31.5 0.8 fusion.44
  32.3 0.7 fusion.52
  32.9 0.7 fusion.43
  34.3 0.7 fusion.42
  35.7 0.7 fusion.41
  36.4 0.7 fusion.55
  37.0 0.7 fusion.45
  38.1 7.5 %collective-permute-done = bf16[2,256,256]{2,1,0:T(8,128)(2,1)S(1)} collective-permute-done((bf16[2,256,256]{2,1,0:T(8,128)(2,1)S(1)}, bf16[2,256,256]{2,1,0:T(8,128)(2,1)S(1)}, u32[]{:S(2)}, u32[]{:S(2)}) %collective-permute-start) | collective-permute-done | bytes 262176 | tf_op jit(solution)/shard_map/while/body/eval_jaxpr/ppermute | solution.py:16
  45.9 1.3 fusion.75
  47.2 1.3 collective-permute-start.1
  48.6 16.3 %collective-permute-done.1 = f32[3,256,256]{2,1,0:T(8,128)S(1)} collective-permute-done((f32[3,256,256]{2,1,0:T(8,128)}, f32[3,256,256]{2,1,0:T(8,128)S(1)}, u32[]{:S(2)}, u32[]{:S(2)}) %collective-permute-start.1) | collective-permute-done | bytes 786464 | tf_op jit(solution)/shard_map/while/body/eval_jaxpr/ppermute | solution.py:27
  64.9 1.2 broadcast_select_fusion.3
  66.4 0.8 concatenate.25
  67.2 16.1 %reduce-scatter.2.cloned.1.call-done = bf16[2,256,256]{2,1,0:T(8,128)(2,1)} async-done(((bf16[4,256,256]{2,1,0:T(8,128)(2,1)}), bf16[2,256,256]{2,1,0:T(8,128)(2,1)}) %reduce-scatter.2.cloned.1.call-update) | async-done | bytes 262160 | tf_op jit(solution)/shard_map/while/body/eval_jaxpr/reduce_scatter | solution.py:145
  83.3 1.0 convert_element_type.136
  84.8 7.5 %collective-permute-done = bf16[2,256,256]{2,1,0:T(8,128)(2,1)S(1)} collective-permute-done((bf16[2,256,256]{2,1,0:T(8,128)(2,1)S(1)}, bf16[2,256,256]{2,1,0:T(8,128)(2,1)S(1)}, u32[]{:S(2)}, u32[]{:S(2)}) %collective-permute-start) | collective-permute-done | bytes 262176 | tf_op jit(solution)/shard_map/while/body/eval_jaxpr/ppermute | solution.py:16
  92.5 1.3 fusion.75
  93.8 10.6 %collective-permute-start.1 = (f32[3,256,256]{2,1,0:T(8,128)}, f32[3,256,256]{2,1,0:T(8,128)S(1)}, u32[]{:S(2)}, u32[]{:S(2)}) collective-permute-start(f32[3,256,256]{2,1,0:T(8,128)} %get-tuple-element.508), channel_id=1, source_target_pairs={{0,4},{4,8},{8,12},{1,5},{5,9},{9,13},{2,6},{6,10},{10,14},{3,7},{... | collective-permute-start | bytes 2359304 | tf_op jit(solution)/shard_map/while/body/eval_jaxpr/ppermute | solution.py:27
  104.4 16.0 %collective-permute-done.1 = f32[3,256,256]{2,1,0:T(8,128)S(1)} collective-permute-done((f32[3,256,256]{2,1,0:T(8,128)}, f32[3,256,256]{2,1,0:T(8,128)S(1)}, u32[]{:S(2)}, u32[]{:S(2)}) %collective-permute-start.1) | collective-permute-done | bytes 786464 | tf_op jit(solution)/shard_map/while/body/eval_jaxpr/ppermute | solution.py:27
  120.4 1.2 broadcast_select_fusion.3
  121.9 0.8 concatenate.25
  122.8 15.8 %reduce-scatter.2.cloned.1.call-done = bf16[2,256,256]{2,1,0:T(8,128)(2,1)} async-done(((bf16[4,256,256]{2,1,0:T(8,128)(2,1)}), bf16[2,256,256]{2,1,0:T(8,128)(2,1)}) %reduce-scatter.2.cloned.1.call-update) | async-done | bytes 262160 | tf_op jit(solution)/shard_map/while/body/eval_jaxpr/reduce_scatter | solution.py:145
  138.6 1.0 convert_element_type.136
  140.0 7.5 %collective-permute-done = bf16[2,256,256]{2,1,0:T(8,128)(2,1)S(1)} collective-permute-done((bf16[2,256,256]{2,1,0:T(8,128)(2,1)S(1)}, bf16[2,256,256]{2,1,0:T(8,128)(2,1)S(1)}, u32[]{:S(2)}, u32[]{:S(2)}) %collective-permute-start) | collective-permute-done | bytes 262176 | tf_op jit(solution)/shard_map/while/body/eval_jaxpr/ppermute | solution.py:16
  147.8 1.3 fusion.75
  149.1 3.4 %collective-permute-start.1 = (f32[3,256,256]{2,1,0:T(8,128)}, f32[3,256,256]{2,1,0:T(8,128)S(1)}, u32[]{:S(2)}, u32[]{:S(2)}) collective-permute-start(f32[3,256,256]{2,1,0:T(8,128)} %get-tuple-element.508), channel_id=1, source_target_pairs={{0,4},{4,8},{8,12},{1,5},{5,9},{9,13},{2,6},{6,10},{10,14},{3,7},{... | collective-permute-start | bytes 2359304 | tf_op jit(solution)/shard_map/while/body/eval_jaxpr/ppermute | solution.py:27
  152.6 16.0 %collective-permute-done.1 = f32[3,256,256]{2,1,0:T(8,128)S(1)} collective-permute-done((f32[3,256,256]{2,1,0:T(8,128)}, f32[3,256,256]{2,1,0:T(8,128)S(1)}, u32[]{:S(2)}, u32[]{:S(2)}) %collective-permute-start.1) | collective-permute-done | bytes 786464 | tf_op jit(solution)/shard_map/while/body/eval_jaxpr/ppermute | solution.py:27
  168.6 1.2 broadcast_select_fusion.3
  170.1 0.8 concatenate.25
  170.9 23.9 %reduce-scatter.2.cloned.1.call-done = bf16[2,256,256]{2,1,0:T(8,128)(2,1)} async-done(((bf16[4,256,256]{2,1,0:T(8,128)(2,1)}), bf16[2,256,256]{2,1,0:T(8,128)(2,1)}) %reduce-scatter.2.cloned.1.call-update) | async-done | bytes 262160 | tf_op jit(solution)/shard_map/while/body/eval_jaxpr/reduce_scatter | solution.py:145
  194.8 1.0 convert_element_type.136
  196.2 7.5 %collective-permute-done = bf16[2,256,256]{2,1,0:T(8,128)(2,1)S(1)} collective-permute-done((bf16[2,256,256]{2,1,0:T(8,128)(2,1)S(1)}, bf16[2,256,256]{2,1,0:T(8,128)(2,1)S(1)}, u32[]{:S(2)}, u32[]{:S(2)}) %collective-permute-start) | collective-permute-done | bytes 262176 | tf_op jit(solution)/shard_map/while/body/eval_jaxpr/ppermute | solution.py:16
  204.0 1.3 fusion.75
  205.3 3.4 %collective-permute-start.1 = (f32[3,256,256]{2,1,0:T(8,128)}, f32[3,256,256]{2,1,0:T(8,128)S(1)}, u32[]{:S(2)}, u32[]{:S(2)}) collective-permute-start(f32[3,256,256]{2,1,0:T(8,128)} %get-tuple-element.508), channel_id=1, source_target_pairs={{0,4},{4,8},{8,12},{1,5},{5,9},{9,13},{2,6},{6,10},{10,14},{3,7},{... | collective-permute-start | bytes 2359304 | tf_op jit(solution)/shard_map/while/body/eval_jaxpr/ppermute | solution.py:27
  208.8 16.0 %collective-permute-done.1 = f32[3,256,256]{2,1,0:T(8,128)S(1)} collective-permute-done((f32[3,256,256]{2,1,0:T(8,128)}, f32[3,256,256]{2,1,0:T(8,128)S(1)}, u32[]{:S(2)}, u32[]{:S(2)}) %collective-permute-start.1) | collective-permute-done | bytes 786464 | tf_op jit(solution)/shard_map/while/body/eval_jaxpr/ppermute | solution.py:27
  224.8 1.0 broadcast_select_fusion.1
  225.8 53.5 %all-reduce.3.cloned.1.call-done = f32[1,3,256,256]{3,2,1,0:T(8,128)} async-done(((f32[1,3,256,256]{3,2,1,0:T(8,128)}), f32[1,3,256,256]{3,2,1,0:T(8,128)}) %all-reduce.3.cloned.1.call-update) | async-done | bytes 786448 | tf_op jit(solution)/shard_map/psum | solution.py:32
  279.3 1.6 constant_dynamic-slice_fusion
  (75 shorter events, 8.0 us)
Async XLA Ops:
  8.1 0.9 copy-start
  8.1 1.0 copy-start.2
  8.1 1.0 copy-start.3
  8.1 1.0 copy-start.4
  9.1 20.4 %reduce-scatter.2.cloned.1.call-start = ((), (), s32[]{:S(2)}) async-start(), calls=%async_computation.2 | async-start | bytes 786432 | tf_op jit(solution)/shard_map/while/body/eval_jaxpr/reduce_scatter | solution.py:145
  37.7 8.0 %collective-permute-start = (bf16[2,256,256]{2,1,0:T(8,128)(2,1)S(1)}, bf16[2,256,256]{2,1,0:T(8,128)(2,1)S(1)}, u32[]{:S(2)}, u32[]{:S(2)}) collective-permute-start(bf16[2,256,256]{2,1,0:T(8,128)(2,1)S(1)} %get-tuple-element.572), channel_id=1, source_target_pairs={{0,2},{2,0},{1,3},{3,1},{4,6},{6,4},{5,7},{7,5},{8,10},{10,8},{9,1... | collective-permute-start | bytes 786440 | tf_op jit(solution)/shard_map/while/body/eval_jaxpr/ppermute | solution.py:16
  47.2 17.7 %collective-permute-start.1 = (f32[3,256,256]{2,1,0:T(8,128)}, f32[3,256,256]{2,1,0:T(8,128)S(1)}, u32[]{:S(2)}, u32[]{:S(2)}) collective-permute-start(f32[3,256,256]{2,1,0:T(8,128)} %get-tuple-element.508), channel_id=1, source_target_pairs={{0,4},{4,8},{8,12},{1,5},{5,9},{9,13},{2,6},{6,10},{10,14},{3,7},{... | collective-permute-start | bytes 2359304 | tf_op jit(solution)/shard_map/while/body/eval_jaxpr/ppermute | solution.py:27
  64.8 18.4 %reduce-scatter.2.cloned.1.call-start = ((), (), s32[]{:S(2)}) async-start(), calls=%async_computation.2 | async-start | bytes 786432 | tf_op jit(solution)/shard_map/while/body/eval_jaxpr/reduce_scatter | solution.py:145
  84.3 7.9 %collective-permute-start = (bf16[2,256,256]{2,1,0:T(8,128)(2,1)S(1)}, bf16[2,256,256]{2,1,0:T(8,128)(2,1)S(1)}, u32[]{:S(2)}, u32[]{:S(2)}) collective-permute-start(bf16[2,256,256]{2,1,0:T(8,128)(2,1)S(1)} %get-tuple-element.572), channel_id=1, source_target_pairs={{0,2},{2,0},{1,3},{3,1},{4,6},{6,4},{5,7},{7,5},{8,10},{10,8},{9,1... | collective-permute-start | bytes 786440 | tf_op jit(solution)/shard_map/while/body/eval_jaxpr/ppermute | solution.py:16
  93.8 26.6 %collective-permute-start.1 = (f32[3,256,256]{2,1,0:T(8,128)}, f32[3,256,256]{2,1,0:T(8,128)S(1)}, u32[]{:S(2)}, u32[]{:S(2)}) collective-permute-start(f32[3,256,256]{2,1,0:T(8,128)} %get-tuple-element.508), channel_id=1, source_target_pairs={{0,4},{4,8},{8,12},{1,5},{5,9},{9,13},{2,6},{6,10},{10,14},{3,7},{... | collective-permute-start | bytes 2359304 | tf_op jit(solution)/shard_map/while/body/eval_jaxpr/ppermute | solution.py:27
  120.4 18.2 %reduce-scatter.2.cloned.1.call-start = ((), (), s32[]{:S(2)}) async-start(), calls=%async_computation.2 | async-start | bytes 786432 | tf_op jit(solution)/shard_map/while/body/eval_jaxpr/reduce_scatter | solution.py:145
  139.6 8.0 %collective-permute-start = (bf16[2,256,256]{2,1,0:T(8,128)(2,1)S(1)}, bf16[2,256,256]{2,1,0:T(8,128)(2,1)S(1)}, u32[]{:S(2)}, u32[]{:S(2)}) collective-permute-start(bf16[2,256,256]{2,1,0:T(8,128)(2,1)S(1)} %get-tuple-element.572), channel_id=1, source_target_pairs={{0,2},{2,0},{1,3},{3,1},{4,6},{6,4},{5,7},{7,5},{8,10},{10,8},{9,1... | collective-permute-start | bytes 786440 | tf_op jit(solution)/shard_map/while/body/eval_jaxpr/ppermute | solution.py:16
  149.1 19.5 %collective-permute-start.1 = (f32[3,256,256]{2,1,0:T(8,128)}, f32[3,256,256]{2,1,0:T(8,128)S(1)}, u32[]{:S(2)}, u32[]{:S(2)}) collective-permute-start(f32[3,256,256]{2,1,0:T(8,128)} %get-tuple-element.508), channel_id=1, source_target_pairs={{0,4},{4,8},{8,12},{1,5},{5,9},{9,13},{2,6},{6,10},{10,14},{3,7},{... | collective-permute-start | bytes 2359304 | tf_op jit(solution)/shard_map/while/body/eval_jaxpr/ppermute | solution.py:27
  168.6 26.3 %reduce-scatter.2.cloned.1.call-start = ((), (), s32[]{:S(2)}) async-start(), calls=%async_computation.2 | async-start | bytes 786432 | tf_op jit(solution)/shard_map/while/body/eval_jaxpr/reduce_scatter | solution.py:145
  195.9 7.9 %collective-permute-start = (bf16[2,256,256]{2,1,0:T(8,128)(2,1)S(1)}, bf16[2,256,256]{2,1,0:T(8,128)(2,1)S(1)}, u32[]{:S(2)}, u32[]{:S(2)}) collective-permute-start(bf16[2,256,256]{2,1,0:T(8,128)(2,1)S(1)} %get-tuple-element.572), channel_id=1, source_target_pairs={{0,2},{2,0},{1,3},{3,1},{4,6},{6,4},{5,7},{7,5},{8,10},{10,8},{9,1... | collective-permute-start | bytes 786440 | tf_op jit(solution)/shard_map/while/body/eval_jaxpr/ppermute | solution.py:16
  205.3 19.5 %collective-permute-start.1 = (f32[3,256,256]{2,1,0:T(8,128)}, f32[3,256,256]{2,1,0:T(8,128)S(1)}, u32[]{:S(2)}, u32[]{:S(2)}) collective-permute-start(f32[3,256,256]{2,1,0:T(8,128)} %get-tuple-element.508), channel_id=1, source_target_pairs={{0,4},{4,8},{8,12},{1,5},{5,9},{9,13},{2,6},{6,10},{10,14},{3,7},{... | collective-permute-start | bytes 2359304 | tf_op jit(solution)/shard_map/while/body/eval_jaxpr/ppermute | solution.py:27
  224.8 1.0 copy-start.1
  224.8 54.5 %all-reduce.3.cloned.1.call-start = ((), (), s32[]{:S(2)}) async-start(), calls=%async_computation.1 | async-start | bytes 1572864 | tf_op jit(solution)/shard_map/psum | solution.py:32
Sparse Core Ops, SparseCore 0:
  15.0 14.4 reduce-scatter.1
  67.9 15.3 reduce-scatter.1
  123.4 15.0 reduce-scatter.1
  171.3 23.4 reduce-scatter.1
Sparse Core Ops, SparseCore 1:
  227.6 51.6 all-reduce.2
